TPU v7x, 256 devices: a whole 4x4x8 slice. The times are simulated.
256 devices in a mesh: prow: 8 (over z), pcol: 32 (over x, y, core).
Axes of the slice: x: 4, y: 4, z: 8, core: 2. Of those that a mesh axis runs over, the one named last changes fastest.
Arguments:
- matrix: bfloat16 [8, 2048, 2, 8192], P(None, 'prow', None, 'pcol'), may hold values from -6 to 6
- pivots: int32 [4, 256], replicated, may hold values from 0 to 16383, as said below
- lower_inverse: bfloat16 [4, 256, 256], replicated, as said below
- upper_inverse: bfloat16 [4, 256, 256], replicated, as said below
Outputs:
- factored: bfloat16 [8, 2048, 2, 8192], P(None, 'prow', None, 'pcol')
Inputs may be any that keep to these rules, and one draw needn't show every extreme that they name: For step s and each i, pivots[s, i] is either s * 256 + i or a row index of s * 256 + 256 or more; the pivots of one step that differ from s * 256 + i are distinct. lower_inverse[s] is unit lower triangular. upper_inverse[s] is upper triangular.
All inputs are finite; a program needn't handle non-finite values.
Results may differ from a plain program's by a relative error of at most 0.0071.
Values may be sent and summed in bfloat16 or wider, within the bound.
A program may use at most 64 MiB of HBM per device.

v0:
```python
import jax
import jax.numpy as jnp
from jax import lax
from jax.sharding import PartitionSpec as P


def spread(value, axis, source):
    kept = jnp.where(lax.axis_index(axis) == source, value, 0).astype(value.dtype)
    return lax.psum(kept, axis)


def local(matrix, pivots, lower_inverse, upper_inverse):
    row_blocks = matrix.shape[0]
    block_size = matrix.shape[1]
    col_blocks = matrix.shape[2]
    local_rows = row_blocks * block_size
    local_cols = col_blocks * block_size
    matrix_loc = matrix.reshape(local_rows, local_cols)
    row_count = lax.axis_size("prow")
    col_count = lax.axis_size("pcol")
    my_row = lax.axis_index("prow")
    my_col = lax.axis_index("pcol")
    row_iota = jnp.arange(local_rows, dtype=jnp.int32)
    col_iota = jnp.arange(local_cols, dtype=jnp.int32)
    global_row = (row_iota // block_size * row_count + my_row) * block_size + row_iota % block_size
    global_col = (col_iota // block_size * col_count + my_col) * block_size + col_iota % block_size
    for step_num in range(pivots.shape[0]):
        begin_at = step_num * block_size
        trail_at = begin_at + block_size
        diag_root = step_num % row_count
        diag_local = step_num // row_count * block_size
        panel_root = step_num % col_count
        panel_local = step_num // col_count * block_size
        targets = begin_at + jnp.arange(block_size, dtype=jnp.int32)
        chosen = pivots[step_num]
        chosen_block = chosen // block_size
        chosen_owner = chosen_block % row_count
        is_mine = chosen_owner == my_row
        chosen_local = chosen_block // row_count * block_size + chosen % block_size
        picked = jnp.take(matrix_loc, jnp.where(is_mine, chosen_local, 0), axis=0)
        picked = jnp.where(is_mine[:, None], picked, jnp.zeros_like(picked))
        diag_rows = matrix_loc[diag_local : diag_local + block_size]
        gathered = lax.all_gather(picked, "prow", axis=0, tiled=True)
        stacked = gathered.reshape(row_count, block_size, local_cols)
        owner_hit = jnp.arange(row_count, dtype=jnp.int32)[:, None] == chosen_owner[None, :]
        new_rows = jnp.sum(
            jnp.where(owner_hit[:, :, None], stacked, jnp.zeros_like(stacked)), axis=0
        )
        old_diag = spread(diag_rows, "prow", diag_root)
        moved_rows = is_mine & (chosen != targets)
        matrix_loc = matrix_loc.at[jnp.where(moved_rows, chosen_local, local_rows)].set(
            old_diag, mode="drop"
        )
        diag_after = matrix_loc[diag_local : diag_local + block_size]
        matrix_loc = matrix_loc.at[diag_local : diag_local + block_size].set(
            jnp.where(my_row == diag_root, new_rows, diag_after)
        )
        upper_full = jnp.dot(
            lower_inverse[step_num], new_rows, preferred_element_type=jnp.float32
        ).astype(jnp.bfloat16)
        col_live = global_col >= trail_at
        upper_use = jnp.where(col_live[None, :], upper_full, jnp.zeros_like(upper_full))
        panel_own = matrix_loc[:, panel_local : panel_local + block_size]
        received = spread(panel_own, "pcol", panel_root)
        left_full = jnp.dot(
            received, upper_inverse[step_num], preferred_element_type=jnp.float32
        ).astype(jnp.bfloat16)
        row_live = global_row >= trail_at
        left_use = jnp.where(row_live[:, None], left_full, jnp.zeros_like(left_full))
        matrix_loc = (
            matrix_loc.astype(jnp.float32)
            - jnp.dot(left_use, upper_use, preferred_element_type=jnp.float32)
        ).astype(jnp.bfloat16)
        panel_now = matrix_loc[:, panel_local : panel_local + block_size]
        panel_put = jnp.where(row_live[:, None] & (my_col == panel_root), left_full, panel_now)
        matrix_loc = matrix_loc.at[:, panel_local : panel_local + block_size].set(panel_put)
        diag_now = matrix_loc[diag_local : diag_local + block_size]
        diag_put = jnp.where(col_live[None, :] & (my_row == diag_root), upper_full, diag_now)
        matrix_loc = matrix_loc.at[diag_local : diag_local + block_size].set(diag_put)
    return matrix_loc.reshape(matrix.shape)


def solution(mesh):
    placed = (P(None, "prow", None, "pcol"), P(), P(), P())
    return jax.shard_map(
        local, mesh=mesh, in_specs=placed, out_specs=P(None, "prow", None, "pcol"), check_vma=False
    )
```

profile of v0, /device:TPU:1, one launch (start us, length us, event | category | flops | bytes accessed | tf_op | source)
XLA Modules:
  0.0 982.3 jit_solution(12199594610326055330)
XLA Ops:
  6.5 1.2 broadcast_select_fusion
  7.7 0.7 copy.18
  8.5 0.9 and_select_fusion
  9.4 2.0 copy.17
  11.5 1.2 gather_fusion
  12.7 0.8 select_select_fusion.7
  13.6 0.7 compare_reduce_fusion
  14.3 0.1 compare_select_fusion
  14.4 66.9 %all-reduce.9.cloned.1.call-done = bf16[256,512]{1,0:T(8,128)(2,1)} async-done(((bf16[256,512]{1,0:T(8,128)(2,1)}), bf16[256,512]{1,0:T(8,128)(2,1)}) %all-reduce.9.cloned.1.call-update) | async-done | bytes 262160 | tf_op jit(solution)/shard_map/psum | solution.py:9
  81.3 3.1 scatter_fusion
  84.4 38.9 %all-gather.5.cloned.1.call-done = bf16[2048,512]{1,0:T(8,128)(2,1)} async-done(((bf16[256,512]{1,0:T(8,128)(2,1)}), bf16[2048,512]{1,0:T(8,128)(2,1)}) %all-gather.5.cloned.1.call-update) | async-done | bytes 2097168 | tf_op jit(solution)/shard_map/all_gather | solution.py:43
  123.4 1.9 select_reduce_fusion.3
  125.3 0.1 fusion.24
  125.3 1.0 slice_select_fusion.3
  126.5 0.2 fusion
  126.7 118.0 %all-reduce.11.cloned.1.call-done = bf16[2048,256]{1,0:T(8,128)(2,1)} async-done(((bf16[2048,256]{1,0:T(8,128)(2,1)}), bf16[2048,256]{1,0:T(8,128)(2,1)}) %all-reduce.11.cloned.1.call-update) | async-done | bytes 1048592 | tf_op jit(solution)/shard_map/psum | solution.py:9
  244.7 1.6 convolution_convert_fusion.3
  246.4 2.0 subtract_convert_fusion.3
  248.4 3.4 fusion.4
  251.8 1.8 broadcast_select_fusion.3
  253.7 3.1 gather_fusion.1
  256.8 0.8 select_select_fusion.6
  257.8 63.7 %all-reduce.13.cloned.1.call-done = bf16[256,512]{1,0:T(8,128)(2,1)} async-done(((bf16[256,512]{1,0:T(8,128)(2,1)}), bf16[256,512]{1,0:T(8,128)(2,1)}) %all-reduce.13.cloned.1.call-update) | async-done | bytes 262160 | tf_op jit(solution)/shard_map/psum | solution.py:9
  321.5 5.2 scatter_fusion.1
  326.7 36.7 %all-gather.7.cloned.1.call-done = bf16[2048,512]{1,0:T(8,128)(2,1)} async-done(((bf16[256,512]{1,0:T(8,128)(2,1)}), bf16[2048,512]{1,0:T(8,128)(2,1)}) %all-gather.7.cloned.1.call-update) | async-done | bytes 2097168 | tf_op jit(solution)/shard_map/all_gather | solution.py:43
  363.4 1.9 select_reduce_fusion.2
  365.2 1.7 fusion.23
  367.0 2.3 slice_select_fusion.2
  369.4 0.2 fusion.1
  369.6 118.0 %all-reduce.15.cloned.1.call-done = bf16[2048,256]{1,0:T(8,128)(2,1)} async-done(((bf16[2048,256]{1,0:T(8,128)(2,1)}), bf16[2048,256]{1,0:T(8,128)(2,1)}) %all-reduce.15.cloned.1.call-update) | async-done | bytes 1048592 | tf_op jit(solution)/shard_map/psum | solution.py:9
  487.6 1.6 convolution_convert_fusion.2
  489.3 2.3 subtract_convert_fusion.2
  491.5 1.5 fusion.5
  493.0 0.8 broadcast_select_fusion.2
  493.8 0.2 all-gather.9.cloned.1.call-start
  494.1 1.2 gather_fusion.2
  495.2 0.8 select_select_fusion.5
  496.2 65.4 %all-reduce.17.cloned.1.call-done = bf16[256,512]{1,0:T(8,128)(2,1)} async-done(((bf16[256,512]{1,0:T(8,128)(2,1)}), bf16[256,512]{1,0:T(8,128)(2,1)}) %all-reduce.17.cloned.1.call-update) | async-done | bytes 262160 | tf_op jit(solution)/shard_map/psum | solution.py:9
  561.6 3.1 scatter_fusion.2
  564.7 38.9 %all-gather.9.cloned.1.call-done = bf16[2048,512]{1,0:T(8,128)(2,1)} async-done(((bf16[256,512]{1,0:T(8,128)(2,1)}), bf16[2048,512]{1,0:T(8,128)(2,1)}) %all-gather.9.cloned.1.call-update) | async-done | bytes 2097168 | tf_op jit(solution)/shard_map/all_gather | solution.py:43
  603.6 1.9 select_reduce_fusion.1
  605.5 0.1 fusion.22
  605.6 1.0 slice_select_fusion.1
  606.8 0.2 fusion.2
  607.0 118.0 %all-reduce.19.cloned.1.call-done = bf16[2048,256]{1,0:T(8,128)(2,1)} async-done(((bf16[2048,256]{1,0:T(8,128)(2,1)}), bf16[2048,256]{1,0:T(8,128)(2,1)}) %all-reduce.19.cloned.1.call-update) | async-done | bytes 1048592 | tf_op jit(solution)/shard_map/psum | solution.py:9
  725.0 1.7 convolution_convert_fusion.1
  726.6 2.0 subtract_convert_fusion.1
  728.6 3.4 fusion.6
  732.0 1.8 broadcast_select_fusion.1
  734.0 3.1 gather_fusion.3
  737.0 0.8 select_select_fusion.4
  738.0 63.7 %all-reduce.21.cloned.1.call-done = bf16[256,512]{1,0:T(8,128)(2,1)} async-done(((bf16[256,512]{1,0:T(8,128)(2,1)}), bf16[256,512]{1,0:T(8,128)(2,1)}) %all-reduce.21.cloned.1.call-update) | async-done | bytes 262160 | tf_op jit(solution)/shard_map/psum | solution.py:9
  801.7 5.2 scatter_fusion.3
  806.9 36.8 %all-gather.11.cloned.1.call-done = bf16[2048,512]{1,0:T(8,128)(2,1)} async-done(((bf16[256,512]{1,0:T(8,128)(2,1)}), bf16[2048,512]{1,0:T(8,128)(2,1)}) %all-gather.11.cloned.1.call-update) | async-done | bytes 2097168 | tf_op jit(solution)/shard_map/all_gather | solution.py:43
  843.8 1.9 select_reduce_fusion
  845.6 1.7 fusion.21
  847.4 2.3 slice_select_fusion
  849.8 0.2 fusion.3
  850.0 118.0 %all-reduce.23.cloned.1.call-done = bf16[2048,256]{1,0:T(8,128)(2,1)} async-done(((bf16[2048,256]{1,0:T(8,128)(2,1)}), bf16[2048,256]{1,0:T(8,128)(2,1)}) %all-reduce.23.cloned.1.call-update) | async-done | bytes 1048592 | tf_op jit(solution)/shard_map/psum | solution.py:9
  968.0 1.6 convolution_convert_fusion
  969.7 2.3 subtract_convert_fusion
  971.9 1.5 fusion.7
  973.4 0.1 fusion.20
  973.5 2.0 reshape.1320
  (53 shorter events, 0.9 us)
Async XLA Ops:
  6.5 74.8 %all-reduce.9.cloned.1.call-start = ((), (), s32[]{:S(2)}) async-start(), calls=%async_computation | async-start | bytes 524288 | tf_op jit(solution)/shard_map/psum | solution.py:9
  8.5 114.9 %all-gather.5.cloned.1.call-start = ((), (), s32[]{:S(2)}) async-start(), calls=%async_computation.1 | async-start | bytes 2359296 | tf_op jit(solution)/shard_map/all_gather | solution.py:43
  11.5 2.8 copy-start.1
  13.5 231.2 %all-reduce.11.cloned.1.call-start = ((), (), s32[]{:S(2)}) async-start(), calls=%async_computation.2 | async-start | bytes 2097152 | tf_op jit(solution)/shard_map/psum | solution.py:9
  125.2 1.3 copy-start
  126.4 195.1 %all-reduce.13.cloned.1.call-start = ((), (), s32[]{:S(2)}) async-start(), calls=%async_computation.3 | async-start | bytes 524288 | tf_op jit(solution)/shard_map/psum | solution.py:9
  253.6 109.7 %all-gather.7.cloned.1.call-start = ((), (), s32[]{:S(2)}) async-start(), calls=%async_computation.4 | async-start | bytes 2359296 | tf_op jit(solution)/shard_map/all_gather | solution.py:43
  257.6 230.0 %all-reduce.15.cloned.1.call-start = ((), (), s32[]{:S(2)}) async-start(), calls=%async_computation.5 | async-start | bytes 2097152 | tf_op jit(solution)/shard_map/psum | solution.py:9
  369.3 192.3 %all-reduce.17.cloned.1.call-start = ((), (), s32[]{:S(2)}) async-start(), calls=%async_computation.6 | async-start | bytes 524288 | tf_op jit(solution)/shard_map/psum | solution.py:9
  493.8 109.8 %all-gather.9.cloned.1.call-start = ((), (), s32[]{:S(2)}) async-start(), calls=%async_computation.7 | async-start | bytes 2359296 | tf_op jit(solution)/shard_map/all_gather | solution.py:43
  496.1 228.9 %all-reduce.19.cloned.1.call-start = ((), (), s32[]{:S(2)}) async-start(), calls=%async_computation.8 | async-start | bytes 2097152 | tf_op jit(solution)/shard_map/psum | solution.py:9
  606.7 195.1 %all-reduce.21.cloned.1.call-start = ((), (), s32[]{:S(2)}) async-start(), calls=%async_computation.9 | async-start | bytes 524288 | tf_op jit(solution)/shard_map/psum | solution.py:9
  733.9 109.9 %all-gather.11.cloned.1.call-start = ((), (), s32[]{:S(2)}) async-start(), calls=%async_computation.10 | async-start | bytes 2359296 | tf_op jit(solution)/shard_map/all_gather | solution.py:43
  737.9 230.1 %all-reduce.23.cloned.1.call-start = ((), (), s32[]{:S(2)}) async-start(), calls=%async_computation.11 | async-start | bytes 2097152 | tf_op jit(solution)/shard_map/psum | solution.py:9
Sparse Core Ops, SparseCore 0:
  9.6 71.6 all-reduce.8
  83.1 40.1 all-gather.4
  126.6 118.0 all-reduce.10
  253.8 67.6 all-reduce.12
  323.1 40.1 all-gather.6
  369.4 118.1 all-reduce.14
  494.0 67.5 all-reduce.16
  563.4 40.1 all-gather.8
  606.9 118.0 all-reduce.18
  734.0 67.6 all-reduce.20
  803.5 40.1 all-gather.10
  849.8 118.1 all-reduce.22
where the time goes:
time: 983 us; the launch traced here: 982 us
  waiting for transfers between devices  883 us (90%)
  other arithmetic  38.6 us (4%)
  local copies, waits for them, and re-layouts  29.8 us (3%)
  matrix products  16 us (2%)
  between operations  13.9 us (1%)
    psum x8, waiting for transfers between devices, spread(): return lax.psum(kept, axis)  732 us
    all_gather x4, waiting for transfers between devices, local(): gathered = lax.all_gather(picked, 'prow', axis=0, tiled=True)  151 us
  transfers between devices with their start and end apart: 12, of which 12 were waited for; matrix products, arithmetic and copies ran while one was open for 3% of the time, Pallas kernels for 0%

commit v1 on v0

--- a/solution.py
+++ b/solution.py
@@ -6,7 +6,7 @@
 
 def spread(value, axis, source):
     kept = jnp.where(lax.axis_index(axis) == source, value, 0).astype(value.dtype)
-    return lax.psum(kept, axis)
+    return jnp.sum(lax.all_gather(kept, axis), axis=0)
 
 
 def local(matrix, pivots, lower_inverse, upper_inverse):

time: 983 us -> 917 us (0.933)
  waiting for transfers between devices: 883 us -> 764 us
  other arithmetic: 38.6 us -> 91.8 us
    psum x8 -> x0, waiting for transfers between devices: 732 us -> none  [spread(): return lax.psum(kept, axis)]
    all_gather x0 -> x8, waiting for transfers between devices: none -> 620 us  [spread(): return jnp.sum(lax.all_gather(kept, axis), axis=0)]
    reduce_sum x0 -> x8, other arithmetic: none -> 53.5 us  [spread(): return jnp.sum(lax.all_gather(kept, axis), axis=0)]
  transfers between devices with their start and end apart: 12 -> 12, of which waited for: 12 -> 12; matrix products, arithmetic and copies ran while one was open for 3% -> 4% of each run, Pallas kernels for 0% -> 0%
where the time goes in v1:
time: 917 us; the launch traced here: 916 us
  waiting for transfers between devices  764 us (83%)
  other arithmetic  91.8 us (10%)
  local copies, waits for them, and re-layouts  28.4 us (3%)
  matrix products  16.5 us (2%)
  between operations  14 us (2%)
    all_gather x8, waiting for transfers between devices, spread(): return jnp.sum(lax.all_gather(kept, axis), axis=0)  620 us
    all_gather x4, waiting for transfers between devices, local(): gathered = lax.all_gather(picked, 'prow', axis=0, tiled=True)  144 us
    reduce_sum x8, other arithmetic, spread(): return jnp.sum(lax.all_gather(kept, axis), axis=0)  53.5 us
  transfers between devices with their start and end apart: 12, of which 12 were waited for; matrix products, arithmetic and copies ran while one was open for 4% of the time, Pallas kernels for 0%

profile of v1, /device:TPU:1, one launch (start us, length us, event | category | flops | bytes accessed | tf_op | source)
XLA Modules:
  0.0 915.7 jit_solution(3823962373879532306)
XLA Ops:
  6.5 0.9 and_select_fusion
  7.5 2.0 copy.21
  9.5 1.2 gather_fusion
  10.7 0.8 select_select_fusion.7
  11.6 1.2 broadcast_select_fusion
  12.8 0.9 select_n.640
  13.8 38.3 %all-gather.22.cloned.1.call-done = bf16[2048,512]{1,0:T(8,128)(2,1)} async-done(((bf16[256,512]{1,0:T(8,128)(2,1)}), bf16[2048,512]{1,0:T(8,128)(2,1)}) %all-gather.22.cloned.1.call-update) | async-done | bytes 2097168 | tf_op jit(solution)/shard_map/all_gather | solution.py:43
  52.1 1.9 select_reduce_fusion.3
  54.0 39.4 %all-gather.20.cloned.1.call-done = bf16[8,256,512]{2,1,0:T(8,128)(2,1)} async-done(((bf16[1,256,512]{2,1,0:T(8,128)(2,1)}), bf16[8,256,512]{2,1,0:T(8,128)(2,1)}) %all-gather.20.cloned.1.call-update) | async-done | bytes 2097168 | tf_op jit(solution)/shard_map/all_gather | solution.py:9
  93.4 2.0 reduce_sum.144
  95.3 2.7 scatter_fusion
  98.1 1.0 slice_select_fusion.3
  100.0 1.1 fusion
  101.1 120.1 %all-gather.30.cloned.1.call-done = bf16[65536,256]{1,0:T(8,128)(2,1)} async-done(((bf16[2048,256]{1,0:T(8,128)(2,1)}), bf16[65536,256]{1,0:T(8,128)(2,1)}) %all-gather.30.cloned.1.call-update) | async-done | bytes 33554448 | tf_op jit(solution)/shard_map/all_gather | solution.py:9
  221.2 11.4 %reduce_sum.146 = bf16[2048,256]{1,0:T(8,128)(2,1)S(1)} reduce(bf16[32,2048,256]{2,1,0:T(8,128)(2,1)} %bitcast.130, bf16[]{:T(256)} %constant.520.clone.1), dimensions={0}, to_apply=%region_3.5 | reduce | flops 16252928 | bytes 34603008 | tf_op jit(solution)/shard_map/reduce_sum | solution.py:9
  232.6 1.3 convolution_convert_fusion.3
  234.0 2.0 subtract_convert_fusion.3
  236.0 3.4 fusion.4
  239.4 1.8 broadcast_select_fusion.3
  241.3 3.1 gather_fusion.1
  244.3 0.8 select_select_fusion.6
  245.3 31.7 %all-gather.32.cloned.1.call-done = bf16[2048,512]{1,0:T(8,128)(2,1)} async-done(((bf16[256,512]{1,0:T(8,128)(2,1)}), bf16[2048,512]{1,0:T(8,128)(2,1)}) %all-gather.32.cloned.1.call-update) | async-done | bytes 2097168 | tf_op jit(solution)/shard_map/all_gather | solution.py:9
  277.0 2.0 reduce_sum.147
  278.9 4.8 scatter_fusion.1
  283.7 34.3 %all-gather.24.cloned.1.call-done = bf16[2048,512]{1,0:T(8,128)(2,1)} async-done(((bf16[256,512]{1,0:T(8,128)(2,1)}), bf16[2048,512]{1,0:T(8,128)(2,1)}) %all-gather.24.cloned.1.call-update) | async-done | bytes 2097168 | tf_op jit(solution)/shard_map/all_gather | solution.py:43
  318.1 1.9 select_reduce_fusion.2
  320.0 1.8 fusion.23
  321.7 2.3 slice_select_fusion.2
  324.6 121.5 %all-gather.34.cloned.1.call-done = bf16[65536,256]{1,0:T(8,128)(2,1)} async-done(((bf16[2048,256]{1,0:T(8,128)(2,1)}), bf16[65536,256]{1,0:T(8,128)(2,1)}) %all-gather.34.cloned.1.call-update) | async-done | bytes 33554448 | tf_op jit(solution)/shard_map/all_gather | solution.py:9
  446.0 11.4 %reduce_sum.149 = bf16[2048,256]{1,0:T(8,128)(2,1)S(1)} reduce(bf16[32,2048,256]{2,1,0:T(8,128)(2,1)} %bitcast.131, bf16[]{:T(256)} %constant.520.clone.1), dimensions={0}, to_apply=%region_8.10 | reduce | flops 16252928 | bytes 34603008 | tf_op jit(solution)/shard_map/reduce_sum | solution.py:9
  457.5 1.3 convolution_convert_fusion.2
  458.8 2.3 subtract_convert_fusion.2
  461.1 1.4 fusion.5
  462.5 0.8 broadcast_select_fusion.2
  463.5 1.2 gather_fusion.2
  464.6 0.8 select_select_fusion.5
  465.5 33.6 %all-gather.36.cloned.1.call-done = bf16[2048,512]{1,0:T(8,128)(2,1)} async-done(((bf16[256,512]{1,0:T(8,128)(2,1)}), bf16[2048,512]{1,0:T(8,128)(2,1)}) %all-gather.36.cloned.1.call-update) | async-done | bytes 2097168 | tf_op jit(solution)/shard_map/all_gather | solution.py:9
  499.2 2.0 reduce_sum.150
  501.1 2.7 scatter_fusion.2
  503.8 36.6 %all-gather.26.cloned.1.call-done = bf16[2048,512]{1,0:T(8,128)(2,1)} async-done(((bf16[256,512]{1,0:T(8,128)(2,1)}), bf16[2048,512]{1,0:T(8,128)(2,1)}) %all-gather.26.cloned.1.call-update) | async-done | bytes 2097168 | tf_op jit(solution)/shard_map/all_gather | solution.py:43
  540.4 1.9 select_reduce_fusion.1
  542.3 1.0 slice_select_fusion.1
  543.8 121.7 %all-gather.38.cloned.1.call-done = bf16[65536,256]{1,0:T(8,128)(2,1)} async-done(((bf16[2048,256]{1,0:T(8,128)(2,1)}), bf16[65536,256]{1,0:T(8,128)(2,1)}) %all-gather.38.cloned.1.call-update) | async-done | bytes 33554448 | tf_op jit(solution)/shard_map/all_gather | solution.py:9
  665.4 11.4 %reduce_sum.152 = bf16[2048,256]{1,0:T(8,128)(2,1)S(1)} reduce(bf16[32,2048,256]{2,1,0:T(8,128)(2,1)} %bitcast.132, bf16[]{:T(256)} %constant.520.clone.1), dimensions={0}, to_apply=%region_12.14 | reduce | flops 16252928 | bytes 34603008 | tf_op jit(solution)/shard_map/reduce_sum | solution.py:9
  676.8 1.3 convolution_convert_fusion.1
  678.2 2.0 subtract_convert_fusion.1
  680.2 3.4 fusion.6
  683.6 1.8 broadcast_select_fusion.1
  685.5 3.1 gather_fusion.3
  688.5 0.8 select_select_fusion.4
  689.5 31.7 %all-gather.40.cloned.1.call-done = bf16[2048,512]{1,0:T(8,128)(2,1)} async-done(((bf16[256,512]{1,0:T(8,128)(2,1)}), bf16[2048,512]{1,0:T(8,128)(2,1)}) %all-gather.40.cloned.1.call-update) | async-done | bytes 2097168 | tf_op jit(solution)/shard_map/all_gather | solution.py:9
  721.2 2.0 reduce_sum.153
  723.1 4.8 scatter_fusion.3
  727.9 34.5 %all-gather.28.cloned.1.call-done = bf16[2048,512]{1,0:T(8,128)(2,1)} async-done(((bf16[256,512]{1,0:T(8,128)(2,1)}), bf16[2048,512]{1,0:T(8,128)(2,1)}) %all-gather.28.cloned.1.call-update) | async-done | bytes 2097168 | tf_op jit(solution)/shard_map/all_gather | solution.py:43
  762.4 1.9 select_reduce_fusion
  764.3 1.7 fusion.21
  766.0 2.3 slice_select_fusion
  768.4 1.1 fusion.3
  769.5 120.8 %all-gather.42.cloned.1.call-done = bf16[65536,256]{1,0:T(8,128)(2,1)} async-done(((bf16[2048,256]{1,0:T(8,128)(2,1)}), bf16[65536,256]{1,0:T(8,128)(2,1)}) %all-gather.42.cloned.1.call-update) | async-done | bytes 33554448 | tf_op jit(solution)/shard_map/all_gather | solution.py:9
  890.3 11.4 %reduce_sum.155 = bf16[2048,256]{1,0:T(8,128)(2,1)S(1)} reduce(bf16[32,2048,256]{2,1,0:T(8,128)(2,1)} %bitcast.133, bf16[]{:T(256)} %constant.520.clone.1), dimensions={0}, to_apply=%region_16.18 | reduce | flops 16252928 | bytes 34603008 | tf_op jit(solution)/shard_map/reduce_sum | solution.py:9
  901.8 1.3 convolution_convert_fusion
  903.1 2.2 subtract_convert_fusion
  905.4 1.4 fusion.7
  906.9 2.0 reshape.1330
  (61 shorter events, 2.6 us)
Async XLA Ops:
  6.5 45.6 %all-gather.22.cloned.1.call-start = ((), (), s32[]{:S(2)}) async-start(), calls=%async_computation.1 | async-start | bytes 2359296 | tf_op jit(solution)/shard_map/all_gather | solution.py:43
  9.5 4.2 copy-start.1
  11.5 81.8 %all-gather.20.cloned.1.call-start = ((), (), s32[]{:S(2)}) async-start(), calls=%async_computation | async-start | bytes 2359296 | tf_op jit(solution)/shard_map/all_gather | solution.py:9
  13.6 207.6 %all-gather.30.cloned.1.call-start = ((), (), s32[]{:S(2)}) async-start(), calls=%async_computation.5 | async-start | bytes 34603008 | tf_op jit(solution)/shard_map/all_gather | solution.py:9
  99.2 177.8 %all-gather.32.cloned.1.call-start = ((), (), s32[]{:S(2)}) async-start(), calls=%async_computation.6 | async-start | bytes 2359296 | tf_op jit(solution)/shard_map/all_gather | solution.py:9
  241.2 76.9 %all-gather.24.cloned.1.call-start = ((), (), s32[]{:S(2)}) async-start(), calls=%async_computation.2 | async-start | bytes 2359296 | tf_op jit(solution)/shard_map/all_gather | solution.py:43
  245.2 200.9 %all-gather.34.cloned.1.call-start = ((), (), s32[]{:S(2)}) async-start(), calls=%async_computation.7 | async-start | bytes 34603008 | tf_op jit(solution)/shard_map/all_gather | solution.py:9
  319.9 4.4 copy-start
  324.0 175.1 %all-gather.36.cloned.1.call-start = ((), (), s32[]{:S(2)}) async-start(), calls=%async_computation.8 | async-start | bytes 2359296 | tf_op jit(solution)/shard_map/all_gather | solution.py:9
  463.4 77.0 %all-gather.26.cloned.1.call-start = ((), (), s32[]{:S(2)}) async-start(), calls=%async_computation.3 | async-start | bytes 2359296 | tf_op jit(solution)/shard_map/all_gather | solution.py:43
  465.5 200.0 %all-gather.38.cloned.1.call-start = ((), (), s32[]{:S(2)}) async-start(), calls=%async_computation.9 | async-start | bytes 34603008 | tf_op jit(solution)/shard_map/all_gather | solution.py:9
  543.4 177.8 %all-gather.40.cloned.1.call-start = ((), (), s32[]{:S(2)}) async-start(), calls=%async_computation.10 | async-start | bytes 2359296 | tf_op jit(solution)/shard_map/all_gather | solution.py:9
  685.4 77.0 %all-gather.28.cloned.1.call-start = ((), (), s32[]{:S(2)}) async-start(), calls=%async_computation.4 | async-start | bytes 2359296 | tf_op jit(solution)/shard_map/all_gather | solution.py:43
  689.4 200.9 %all-gather.42.cloned.1.call-start = ((), (), s32[]{:S(2)}) async-start(), calls=%async_computation.11 | async-start | bytes 34603008 | tf_op jit(solution)/shard_map/all_gather | solution.py:9
Sparse Core Ops, SparseCore 0:
  11.7 40.4 all-gather.21
  53.9 39.4 all-gather.19
  99.3 121.8 all-gather.29
  241.3 35.6 all-gather.31
  278.6 39.4 all-gather.23
  324.2 121.8 all-gather.33
  463.5 35.6 all-gather.35
  500.9 39.4 all-gather.25
  543.5 121.8 all-gather.37
  685.5 35.6 all-gather.39
  723.0 39.4 all-gather.27
  768.4 121.8 all-gather.41
